TPU v7x, 128 devices: a whole 4x4x4 slice. The times are simulated.
128 devices in a mesh: dp: 2 (over z_lo), head: 8 (over z_hi, y), tensor: 8 (over x, core).
Axes of the slice: x: 4, y: 4, z: 4 (z_hi: 2, z_lo: 2; z = z_hi * 2 + z_lo), core: 2. Of those that a mesh axis runs over, the one named last changes fastest.
Arguments:
- tokens: bfloat16 [512, 8192], P('dp', 'tensor'), may hold values from -6 to 6
- cotangent: bfloat16 [512, 8192], P('dp', 'tensor'), may hold values from -6 to 6
- w_gate: bfloat16 [8192, 29568], P('tensor', 'head'), may hold values from -0.0625 to 0.0625
- w_up: bfloat16 [8192, 29568], P('tensor', 'head'), may hold values from -0.0625 to 0.0625
- w_down: bfloat16 [29568, 8192], P('head', 'tensor'), may hold values from -0.03125 to 0.03125
- common_down_factor: bfloat16 [8192, 64], P('tensor'), may hold values from -0.0625 to 0.0625
- head_up: bfloat16 [64, 64, 8192], P('head', None, 'tensor'), may hold values from -0.0625 to 0.0625
- routes: int32 [512, 1], P('dp'), may hold values from 0 to 63
Outputs:
- grad_x: bfloat16 [512, 8192], P(('dp', 'head'), 'tensor')
- grad_shared: float32 [8192, 64], P('tensor')
- up_head_gradients: float32 [64, 64, 8192], P('head', None, 'tensor')
Inputs may be any that keep to these rules, and one draw needn't show every extreme that they name: `routes`: each token names one adapter head; the loads are skewed.
All inputs are finite; a program needn't handle non-finite values.
Results may differ from a plain program's by a relative error of at most 0.015.
Values may be sent and summed in bfloat16 or wider, within the bound.
A program may use at most 128 MiB of HBM per device.

v0:
```python
import jax
import jax.numpy as jnp
from jax import lax
from jax.sharding import PartitionSpec as P

ADAPTER_SCALE = 2.0


def contract_last(left, right):
    return lax.dot_general(
        left, right, (((1,), (1,)), ((), ())), preferred_element_type=jnp.float32
    )


def local(tokens, cotangent, w_gate, w_up, w_down, common_down_factor, head_up, routes):
    tok_rows, d_cols = tokens.shape
    hidden_activation = w_gate.shape[1]
    reduced_activation = common_down_factor.shape[1]
    local_heads = head_up.shape[0]
    first_head = lax.axis_index("head") * local_heads
    assigned_mask = (
        routes == first_head + jnp.arange(local_heads, dtype=jnp.int32)[None, :]
    ).astype(jnp.float32)
    flat_heads = head_up.reshape(local_heads * reduced_activation, d_cols)
    gate_preactivation = jnp.dot(tokens, w_gate, preferred_element_type=jnp.float32)
    up_preactivation = jnp.dot(tokens, w_up, preferred_element_type=jnp.float32)
    returned_gradient = contract_last(cotangent, w_down)
    adapter_selectors = jnp.dot(tokens, common_down_factor, preferred_element_type=jnp.float32)
    head_separated = contract_last(cotangent, flat_heads).reshape(
        tok_rows, local_heads, reduced_activation
    )
    selector_gradient = ADAPTER_SCALE * jnp.sum(head_separated * assigned_mask[:, :, None], axis=1)
    combined_total = lax.psum(
        jnp.concatenate(
            [
                gate_preactivation,
                up_preactivation,
                returned_gradient,
                adapter_selectors,
                selector_gradient,
            ],
            axis=1,
        ),
        "tensor",
    )
    gate_preactivation = combined_total[:, :hidden_activation]
    up_preactivation = combined_total[:, hidden_activation : 2 * hidden_activation]
    returned_gradient = combined_total[:, 2 * hidden_activation : 3 * hidden_activation]
    adapter_selectors = combined_total[
        :, 3 * hidden_activation : 3 * hidden_activation + reduced_activation
    ].astype(jnp.bfloat16)
    selector_gradient = combined_total[:, 3 * hidden_activation + reduced_activation :].astype(
        jnp.bfloat16
    )
    sig_gate = jax.nn.sigmoid(gate_preactivation)
    gate_gradient = (
        returned_gradient
        * up_preactivation
        * sig_gate
        * (1.0 + gate_preactivation * (1.0 - sig_gate))
    ).astype(jnp.bfloat16)
    up_gradient = (returned_gradient * gate_preactivation * sig_gate).astype(jnp.bfloat16)
    gate_gradient, up_gradient, adapter_selectors, selector_gradient = (
        gate_gradient,
        up_gradient,
        adapter_selectors,
        selector_gradient,
    )
    ffn_part = contract_last(gate_gradient, w_gate) + contract_last(up_gradient, w_up)
    own_ffn, own_code = (
        lax.psum_scatter(ffn_part, "head", scatter_dimension=0, tiled=True),
        lax.psum_scatter(
            selector_gradient.astype(jnp.float32), "head", scatter_dimension=0, tiled=True
        ),
    )
    grad_x = (own_ffn + contract_last(own_code.astype(jnp.bfloat16), common_down_factor)).astype(
        jnp.bfloat16
    )
    selector_mask = (
        adapter_selectors[:, None, :] * assigned_mask[:, :, None].astype(jnp.bfloat16)
    ).reshape(tok_rows, local_heads * reduced_activation)
    head_contributions = ADAPTER_SCALE * lax.dot_general(
        selector_mask, cotangent, (((0,), (0,)), ((), ())), preferred_element_type=jnp.float32
    )
    up_head_gradients = lax.psum(
        head_contributions.reshape(local_heads, reduced_activation, d_cols).astype(jnp.bfloat16),
        "dp",
    ).astype(jnp.float32)
    shared_term = lax.dot_general(
        tokens, selector_gradient, (((0,), (0,)), ((), ())), preferred_element_type=jnp.float32
    )
    grad_shared = lax.psum(shared_term.astype(jnp.bfloat16), ("dp", "head")).astype(jnp.float32)
    return (grad_x, grad_shared, up_head_gradients)


def solution(mesh):
    placed = (
        P("dp", "tensor"),
        P("dp", "tensor"),
        P("tensor", "head"),
        P("tensor", "head"),
        P("head", "tensor"),
        P("tensor", None),
        P("head", None, "tensor"),
        P("dp", None),
    )
    return jax.shard_map(
        local,
        mesh=mesh,
        in_specs=placed,
        out_specs=(P(("dp", "head"), "tensor"), P("tensor", None), P("head", None, "tensor")),
        check_vma=False,
    )
```

profile of v0, /device:TPU:0, one launch (start us, length us, event | category | flops | bytes accessed | tf_op | source)
XLA Modules:
  0.0 459.9 jit_solution(7197060639671306123)
XLA Ops:
  7.3 0.9 fusion.15
  8.2 7.9 %convolution_dynamic-update-slice_fusion.2 = f32[256,11216]{0,1:T(8,128)} fusion(bf16[256,1024]{1,0:T(8,128)(2,1)} %param.8, bf16[1024,3696]{0,1:T(8,128)(2,1)} %param.10), kind=kOutput, calls=%fused_computation.2 | convolution fusion | flops 1937768448 | bytes 11878400 | tf_op jit(solution)/shard_map/dot_general | solution.py:25
  16.1 4.3 convolution_dynamic-update-slice_fusion.1
  20.4 0.5 fusion.9
  20.9 4.3 convolution_dynamic-update-slice_fusion
  25.2 0.9 convolution_dynamic-update-slice_fusion.3
  26.1 0.6 multiply_dynamic-update-slice_fusion
  26.8 135.7 %all-reduce.4.cloned.1.call-done = f32[256,11216]{0,1:T(8,128)} async-done(((f32[256,11216]{0,1:T(8,128)}), f32[256,11216]{0,1:T(8,128)}) %all-reduce.4.cloned.1.call-update) | async-done | bytes 11485200 | tf_op jit(solution)/shard_map/psum | solution.py:33
  162.5 4.8 %convert.4 = bf16[256,11216]{0,1:T(8,128)(2,1)S(1)} convert(f32[256,11216]{0,1:T(8,128)} %all-reduce.4.cloned.1.call-done) | non-fusion elementwise | flops 2871296 | bytes 17227776 | tf_op jit(solution)/shard_map/convert.1
  167.4 2.4 copy-done.1
  169.8 0.9 fusion.10
  170.7 0.8 fusion.18
  171.5 0.8 copy.13
  172.4 1.4 multiply_convert_fusion.1
  174.1 7.7 %fusion.3 = f32[256,1024]{1,0:T(8,128)S(1)} fusion(bf16[1024,3696]{0,1:T(8,128)(2,1)} %param.11, f32[256,11216]{0,1:T(8,128)} %all-reduce.4.cloned.1.call-done), kind=kOutput, calls=%fused_computation.10 | convolution fusion | flops 1943445504 | bytes 16187392 | tf_op jit(solution)/shard_map/dot_general | solution.py:10
  181.7 10.2 %fusion.6 = f32[256,1024]{1,0:T(8,128)} fusion(f32[256,1024]{1,0:T(8,128)S(1)} %fusion.3, bf16[1024,3696]{0,1:T(8,128)(2,1)} %param.10, f32[256,11216]{0,1:T(8,128)} %all-reduce.4.cloned.1.call-done), kind=kOutput, calls=%fused_computation.12 | convolution fusion | flops 1947492352 | bytes 21020672 | tf_op jit(solution)/shard_map/dot_general | solution.py:10
  192.0 61.1 %all-reduce.6.cloned.1.call-done = bf16[1024,64]{0,1:T(8,128)(2,1)} async-done(((bf16[1024,64]{0,1:T(8,128)(2,1)}), bf16[1024,64]{0,1:T(8,128)(2,1)}) %all-reduce.6.cloned.1.call-update) | async-done | bytes 131088 | tf_op jit(solution)/shard_map/psum | solution.py:92
  253.1 1.6 convert_element_type.61
  254.7 71.5 %reduce-scatter.7.cloned.1.call-done = f32[32,64]{1,0:T(8,128)} async-done(((f32[256,64]{1,0:T(8,128)}), f32[32,64]{1,0:T(8,128)}) %reduce-scatter.7.cloned.1.call-update) | async-done | bytes 8208
  326.2 0.8 copy.14
  327.0 48.0 %all-reduce.8.cloned.1.call-done = bf16[8,64,1024]{2,1,0:T(8,128)(2,1)} async-done(((bf16[8,64,1024]{2,1,0:T(8,128)(2,1)}), bf16[8,64,1024]{2,1,0:T(8,128)(2,1)}) %all-reduce.8.cloned.1.call-update) | async-done | bytes 1048592 | tf_op jit(solution)/shard_map/psum | solution.py:85
  375.0 2.8 convert_element_type.65
  377.8 73.9 %reduce-scatter.5.cloned.1.call-done = f32[32,1024]{1,0:T(8,128)} async-done(((f32[256,1024]{1,0:T(8,128)}), f32[32,1024]{1,0:T(8,128)}) %reduce-scatter.5.cloned.1.call-update) | async-done | bytes 131088 | tf_op jit(solution)/shard_map/reduce_scatter | solution.py:71
  451.7 1.7 fusion.11
  (28 shorter events, 0.5 us)
Async XLA Ops:
  7.2 13.2 %copy-start = (bf16[8,64,1024]{2,1,0:T(8,128)(2,1)S(1)}, bf16[8,64,1024]{2,1,0:T(8,128)(2,1)}, u32[]{:S(2)}) copy-start(bf16[8,64,1024]{2,1,0:T(8,128)(2,1)} %param.14) | copy-start | bytes 3145732
  7.2 8.9 %copy-start.2 = (bf16[256,1024]{1,0:T(8,128)(2,1)S(1)}, bf16[256,1024]{1,0:T(8,128)(2,1)}, u32[]{:S(2)}) copy-start(bf16[256,1024]{1,0:T(8,128)(2,1)} %param.8) | copy-start | bytes 1572868
  7.2 155.3 %all-reduce.4.cloned.1.call-start = ((), (), s32[]{:S(2)}) async-start(), calls=%async_computation.2 | async-start | bytes 22970368 | tf_op jit(solution)/shard_map/psum | solution.py:33
  7.2 8.8 %copy-start.5 = (bf16[1024,3696]{0,1:T(8,128)(2,1)S(1)}, bf16[1024,3696]{0,1:T(8,128)(2,1)}, u32[]{:S(2)}) copy-start(bf16[1024,3696]{0,1:T(8,128)(2,1)} %param.11) | copy-start | bytes 22708228
  8.2 12.7 %slice-start = ((s8[7569408]{0:T(1024)(128)(4,1)}), s8[4194304]{0:T(1024)(128)(4,1)S(1)}, s32[]{:S(2)}) async-start(s8[7569408]{0:T(1024)(128)(4,1)} %bitcast.28), calls=%async_computation.7 | async-start | bytes 8388608
  16.1 4.3 copy-start.3
  16.1 4.8 %slice-start.1 = ((s8[7569408]{0:T(1024)(128)(4,1)}), s8[3375104]{0:T(1024)(128)(4,1)S(1)}, s32[]{:S(2)}) async-start(s8[7569408]{0:T(1024)(128)(4,1)} %bitcast.28), calls=%async_computation.8 | async-start | bytes 6750208
  20.4 4.8 %copy-start.4 = (bf16[1024,64]{0,1:T(8,128)(2,1)S(1)}, bf16[1024,64]{0,1:T(8,128)(2,1)}, u32[]{:S(2)}) copy-start(bf16[1024,64]{0,1:T(8,128)(2,1)} %param.13) | copy-start | bytes 393220
  26.8 226.4 %all-reduce.6.cloned.1.call-start = ((), (), s32[]{:S(2)}) async-start(), calls=%async_computation.4 | async-start | bytes 262144 | tf_op jit(solution)/shard_map/psum | solution.py:92
  167.4 2.5 copy-start.1
  170.7 155.5 %reduce-scatter.7.cloned.1.call-start = ((), (), s32[]{:S(2)}) async-start(), calls=%async_computation.6 | async-start | bytes 147456
  172.3 202.7 %all-reduce.8.cloned.1.call-start = ((), (), s32[]{:S(2)}) async-start(), calls=%async_computation.5 | async-start | bytes 2097152 | tf_op jit(solution)/shard_map/psum | solution.py:85
  173.8 277.9 %reduce-scatter.5.cloned.1.call-start = ((), (), s32[]{:S(2)}) async-start(), calls=%async_computation.3 | async-start | bytes 1179648 | tf_op jit(solution)/shard_map/reduce_scatter | solution.py:71
Sparse Core Ops, SparseCore 0:
  26.9 135.6 all-reduce.3
  170.8 82.2 all-reduce.5
  257.1 69.0 reduce-scatter.6
  329.2 45.7 all-reduce.7
  378.5 73.1 reduce-scatter.4
where the time goes:
time: 460 us
  waiting for transfers between devices  390 us (85%)
  matrix products  39.8 us (9%)
  between operations  13.9 us (3%)
  other arithmetic  11.6 us (3%)
    psum x1, waiting for transfers between devices, local(): lax.psum(jnp.concatenate([gate_preactivation, up_preactivation, returned_...  136 us
    reduce_scatter x1, waiting for transfers between devices, local(): lax.psum_scatter(ffn_part, 'head', scatter_dimension=0, tiled=True)  73.9 us
    unnamed x6, waiting for transfers between devices  71.5 us
    psum x1, waiting for transfers between devices, local(): lax.psum(shared_term.astype(jnp.bfloat16), ('dp', 'head'))  61.1 us
    psum x1, waiting for transfers between devices, local(): lax.psum(head_contributions.reshape(local_heads, reduced_activation, d_co...  48 us
    dot_general x5, matrix products, contract_last(): lax.dot_general(left, right, (((1,), (1,)), ((), ())), preferred_element_...  24.4 us
  transfers between devices with their start and end apart: 5, of which 5 were waited for; matrix products, arithmetic and copies ran while one was open for 6% of the time, Pallas kernels for 0%

commit v1 on v0

--- a/solution.py
+++ b/solution.py
@@ -30,27 +30,21 @@
         tok_rows, local_heads, reduced_activation
     )
     selector_gradient = ADAPTER_SCALE * jnp.sum(head_separated * assigned_mask[:, :, None], axis=1)
-    combined_total = lax.psum(
-        jnp.concatenate(
-            [
-                gate_preactivation,
-                up_preactivation,
-                returned_gradient,
-                adapter_selectors,
-                selector_gradient,
-            ],
-            axis=1,
-        ),
-        "tensor",
+    partial = jnp.concatenate(
+        [
+            gate_preactivation.astype(jnp.bfloat16),
+            up_preactivation.astype(jnp.bfloat16),
+            returned_gradient.astype(jnp.bfloat16),
+            adapter_selectors.astype(jnp.bfloat16),
+            selector_gradient.astype(jnp.bfloat16),
+        ],
+        axis=1,
     )
-    gate_preactivation = combined_total[:, :hidden_activation]
-    up_preactivation = combined_total[:, hidden_activation : 2 * hidden_activation]
-    returned_gradient = combined_total[:, 2 * hidden_activation : 3 * hidden_activation]
-    adapter_selectors = combined_total[
-        :, 3 * hidden_activation : 3 * hidden_activation + reduced_activation
-    ].astype(jnp.bfloat16)
-    selector_gradient = combined_total[:, 3 * hidden_activation + reduced_activation :].astype(
-        jnp.bfloat16
+    own_rows = lax.psum_scatter(partial, "tensor", scatter_dimension=0, tiled=True)
+    gate_preactivation = own_rows[:, :hidden_activation].astype(jnp.float32)
+    up_preactivation = own_rows[:, hidden_activation : 2 * hidden_activation].astype(jnp.float32)
+    returned_gradient = own_rows[:, 2 * hidden_activation : 3 * hidden_activation].astype(
+        jnp.float32
     )
     sig_gate = jax.nn.sigmoid(gate_preactivation)
     gate_gradient = (
@@ -60,21 +54,25 @@
         * (1.0 + gate_preactivation * (1.0 - sig_gate))
     ).astype(jnp.bfloat16)
     up_gradient = (returned_gradient * gate_preactivation * sig_gate).astype(jnp.bfloat16)
-    gate_gradient, up_gradient, adapter_selectors, selector_gradient = (
-        gate_gradient,
-        up_gradient,
-        adapter_selectors,
-        selector_gradient,
+    gathered = lax.all_gather(
+        jnp.concatenate([gate_gradient, up_gradient, own_rows[:, 3 * hidden_activation :]], axis=1),
+        "tensor",
+        axis=0,
+        tiled=True,
     )
-    ffn_part = contract_last(gate_gradient, w_gate) + contract_last(up_gradient, w_up)
-    own_ffn, own_code = (
-        lax.psum_scatter(ffn_part, "head", scatter_dimension=0, tiled=True),
-        lax.psum_scatter(
-            selector_gradient.astype(jnp.float32), "head", scatter_dimension=0, tiled=True
-        ),
+    gate_gradient = gathered[:, :hidden_activation]
+    up_gradient = gathered[:, hidden_activation : 2 * hidden_activation]
+    adapter_selectors = gathered[
+        :, 2 * hidden_activation : 2 * hidden_activation + reduced_activation
+    ]
+    selector_gradient = gathered[:, 2 * hidden_activation + reduced_activation :]
+    ffn_part = (
+        contract_last(gate_gradient, w_gate)
+        + contract_last(up_gradient, w_up)
+        + contract_last(selector_gradient, common_down_factor)
     )
-    grad_x = (own_ffn + contract_last(own_code.astype(jnp.bfloat16), common_down_factor)).astype(
-        jnp.bfloat16
+    grad_x = lax.psum_scatter(
+        ffn_part.astype(jnp.bfloat16), "head", scatter_dimension=0, tiled=True
     )
     selector_mask = (
         adapter_selectors[:, None, :] * assigned_mask[:, :, None].astype(jnp.bfloat16)

time: 460 us -> 328 us (0.71)
  waiting for transfers between devices: 390 us -> 263 us
  matrix products: 39.8 us -> 31.2 us
  local copies, waits for them, and re-layouts: 4.05 us -> 11.4 us
    psum x1 -> x0, waiting for transfers between devices: 136 us -> none  [local(): lax.psum(jnp.concatenate([gate_preactivation, up_preactivation, returned_...]
    unnamed x6 -> x5, waiting for transfers between devices: 71.5 us -> 0.08 us
    reduce_scatter x1 -> x2, waiting for transfers between devices: 73.9 us -> 117 us  [the longest x1 73.1 us: local(): lax.psum_scatter(ffn_part.astype(jnp.bfloat16), 'head', scatter_dimension...]
    all_gather x0 -> x1, waiting for transfers between devices: none -> 30.3 us  [local(): lax.all_gather(jnp.concatenate([gate_gradient, up_gradient, own_rows[:, 3...]
    dot_general x5, matrix products: 24.4 us -> 16.7 us  [contract_last(): lax.dot_general(left, right, (((1,), (1,)), ((), ())), preferred_element_...]
    psum x1, waiting for transfers between devices: 61.1 us -> 68.6 us  [local(): lax.psum(shared_term.astype(jnp.bfloat16), ('dp', 'head'))]
    another operation x1 -> x0, other arithmetic: 4.81 us -> none
where the time goes in v1:
time: 328 us
  waiting for transfers between devices  263 us (80%)
  matrix products  31.2 us (10%)
  between operations  13.9 us (4%)
  local copies, waits for them, and re-layouts  11.4 us (3%)
  other arithmetic  7.4 us (2%)
    reduce_scatter x1, waiting for transfers between devices, local(): lax.psum_scatter(ffn_part.astype(jnp.bfloat16), 'head', scatter_dimension...  73.1 us
    psum x1, waiting for transfers between devices, local(): lax.psum(shared_term.astype(jnp.bfloat16), ('dp', 'head'))  68.6 us
    psum x1, waiting for transfers between devices, local(): lax.psum(head_contributions.reshape(local_heads, reduced_activation, d_co...  47.5 us
    reduce_scatter x1, waiting for transfers between devices, local(): lax.psum_scatter(partial, 'tensor', scatter_dimension=0, tiled=True)  43.7 us
    all_gather x1, waiting for transfers between devices, local(): lax.all_gather(jnp.concatenate([gate_gradient, up_gradient, own_rows[:, 3...  30.3 us
    dot_general x5, matrix products, contract_last(): lax.dot_general(left, right, (((1,), (1,)), ((), ())), preferred_element_...  16.7 us
    unnamed x17, local copies, waits for them, and re-layouts  8.5 us
    dot_general x1, matrix products, local(): jnp.dot(tokens, w_gate, preferred_element_type=jnp.float32)  6.88 us
  transfers between devices with their start and end apart: 5, of which 5 were waited for; matrix products, arithmetic and copies ran while one was open for 6% of the time, Pallas kernels for 0%

profile of v1, /device:TPU:0, one launch (start us, length us, event | category | flops | bytes accessed | tf_op | source)
XLA Modules:
  0.0 327.6 jit_solution(7032396311072623166)
XLA Ops:
  7.2 0.8 fusion.27
  8.1 6.9 %fusion.2 = bf16[256,11216]{0,1:T(8,128)(2,1)} fusion(bf16[256,1024]{1,0:T(8,128)(2,1)} %param.8, bf16[1024,3696]{0,1:T(8,128)(2,1)} %param.10), kind=kOutput, calls=%fused_computation.5 | convolution fusion | flops 1938714624 | bytes 9986048 | tf_op jit(solution)/shard_map/dot_general | solution.py:25
  15.0 3.5 %fusion.1 = bf16[256,11216]{0,1:T(8,128)(2,1)} fusion(bf16[256,11216]{0,1:T(8,128)(2,1)} %fusion.2, bf16[256,1024]{1,0:T(8,128)(2,1)S(1)} %copy-done.1, bf16[1024,3696]{0,1:T(8,128)(2,1)S(1)} %copy-done.5), kind=kOutput, calls=%fused_computation.3 | convolution fusion | flops 1938714624 | bytes 9986048 | tf_op jit(solution)/shard_map/dot_general | solution.py:26
  18.5 0.5 fusion.11
  19.0 3.4 %fusion = bf16[256,11216]{0,1:T(8,128)(2,1)} fusion(bf16[256,11216]{0,1:T(8,128)(2,1)} %fusion.1, bf16[256,1024]{1,0:T(8,128)(2,1)S(1)} %copy-done.2, bf16[3696,1024]{1,0:T(8,128)(2,1)S(1)} %bitcast.28), kind=kOutput, calls=%fused_computation.1 | convolution fusion | flops 1938714624 | bytes 9986048 | tf_op jit(solution)/shard_map/dot_general | solution.py:10
  22.5 0.9 fusion.13
  23.4 0.6 fusion.26
  24.0 8.5 %copy.22 = bf16[256,11216]{1,0:T(8,128)(2,1)} copy(bf16[256,11216]{0,1:T(8,128)(2,1)} %fusion.26) | data formatting | bytes 11485184
  32.5 43.7 %reduce-scatter.7.cloned.1.call-done = bf16[32,11216]{1,0:T(8,128)(2,1)} async-done(((bf16[256,11216]{1,0:T(8,128)(2,1)}), bf16[32,11216]{1,0:T(8,128)(2,1)}) %reduce-scatter.7.cloned.1.call-update) | async-done | bytes 717840 | tf_op jit(solution)/shard_map/reduce_scatter | solution.py:43
  76.2 0.8 slice.35
  77.0 1.5 fusion.23
  78.6 1.0 concatenate.7
  79.7 30.3 %all-gather.2.cloned.1.call-done = bf16[256,7520]{1,0:T(8,128)(2,1)} async-done(((bf16[32,7520]{1,0:T(8,128)(2,1)}), bf16[256,7520]{1,0:T(8,128)(2,1)}) %all-gather.2.cloned.1.call-update) | async-done | bytes 3850256 | tf_op jit(solution)/shard_map/all_gather | solution.py:57
  110.0 1.0 slice.39
  111.1 1.8 fusion.12
  113.0 1.4 multiply_convert_fusion
  114.7 6.1 %fusion.3 = f32[256,1024]{1,0:T(8,128)S(1)} fusion(bf16[1024,3696]{0,1:T(8,128)(2,1)} %param.11, bf16[256,7520]{1,0:T(8,128)(2,1)} %all-gather.2.cloned.1.call-done), kind=kOutput, calls=%fused_computation.7 | convolution fusion | flops 1937768448 | bytes 10518528 | tf_op jit(solution)/shard_map/dot_general | solution.py:10
  120.8 5.5 %fusion.7 = f32[256,1024]{1,0:T(8,128)S(1)} fusion(f32[256,1024]{1,0:T(8,128)S(1)} %fusion.3, bf16[1024,3696]{0,1:T(8,128)(2,1)} %param.10, bf16[256,7520]{1,0:T(8,128)(2,1)S(1)} %copy-done.4), kind=kOutput, calls=%fused_computation.12 | convolution fusion | flops 1938030592 | bytes 11567104 | tf_op jit(solution)/shard_map/dot_general | solution.py:10
  126.3 1.1 fusion.10
  127.5 68.6 %all-reduce.3.cloned.1.call-done = bf16[1024,64]{0,1:T(8,128)(2,1)} async-done(((bf16[1024,64]{0,1:T(8,128)(2,1)}), bf16[1024,64]{0,1:T(8,128)(2,1)}) %all-reduce.3.cloned.1.call-update) | async-done | bytes 131088 | tf_op jit(solution)/shard_map/psum | solution.py:90
  196.1 1.6 convert_element_type.83
  197.8 47.5 %all-reduce.5.cloned.1.call-done = bf16[8,64,1024]{2,1,0:T(8,128)(2,1)} async-done(((bf16[8,64,1024]{2,1,0:T(8,128)(2,1)}), bf16[8,64,1024]{2,1,0:T(8,128)(2,1)}) %all-reduce.5.cloned.1.call-update) | async-done | bytes 1048592 | tf_op jit(solution)/shard_map/psum | solution.py:83
  245.2 2.8 convert_element_type.87
  248.0 73.1 %reduce-scatter.5.cloned.1.call-done = bf16[32,1024]{1,0:T(8,128)(2,1)} async-done(((bf16[256,1024]{1,0:T(8,128)(2,1)}), bf16[32,1024]{1,0:T(8,128)(2,1)}) %reduce-scatter.5.cloned.1.call-update) | async-done | bytes 65552 | tf_op jit(solution)/shard_map/reduce_scatter | solution.py:74
  (30 shorter events, 0.6 us)
Async XLA Ops:
  7.2 11.3 %copy-start = (bf16[8,64,1024]{2,1,0:T(8,128)(2,1)S(1)}, bf16[8,64,1024]{2,1,0:T(8,128)(2,1)}, u32[]{:S(2)}) copy-start(bf16[8,64,1024]{2,1,0:T(8,128)(2,1)} %param.14) | copy-start | bytes 3145732
  7.2 69.1 %reduce-scatter.7.cloned.1.call-start = ((), (), s32[]{:S(2)}) async-start(), calls=%async_computation.6 | async-start | bytes 6488064 | tf_op jit(solution)/shard_map/reduce_scatter | solution.py:43
  8.1 6.9 %copy-start.1 = (bf16[256,1024]{1,0:T(8,128)(2,1)S(1)}, bf16[256,1024]{1,0:T(8,128)(2,1)}, u32[]{:S(2)}) copy-start(bf16[256,1024]{1,0:T(8,128)(2,1)} %param.8) | copy-start | bytes 1572868
  8.1 6.9 %copy-start.5 = (bf16[1024,3696]{0,1:T(8,128)(2,1)S(1)}, bf16[1024,3696]{0,1:T(8,128)(2,1)}, u32[]{:S(2)}) copy-start(bf16[1024,3696]{0,1:T(8,128)(2,1)} %param.11) | copy-start | bytes 22708228
  8.1 10.9 %slice-start = ((s8[7569408]{0:T(1024)(128)(4,1)}), s8[4194304]{0:T(1024)(128)(4,1)S(1)}, s32[]{:S(2)}) async-start(s8[7569408]{0:T(1024)(128)(4,1)} %bitcast.27), calls=%async_computation.7 | async-start | bytes 8388608
  15.0 3.5 %copy-start.2 = (bf16[256,1024]{1,0:T(8,128)(2,1)S(1)}, bf16[256,1024]{1,0:T(8,128)(2,1)}, u32[]{:S(2)}) copy-start(bf16[256,1024]{1,0:T(8,128)(2,1)} %param.9) | copy-start | bytes 1572868
  15.0 4.0 %slice-start.1 = ((s8[7569408]{0:T(1024)(128)(4,1)}), s8[3375104]{0:T(1024)(128)(4,1)S(1)}, s32[]{:S(2)}) async-start(s8[7569408]{0:T(1024)(128)(4,1)} %bitcast.27), calls=%async_computation.8 | async-start | bytes 6750208
  19.0 3.5 %copy-start.3 = (bf16[1024,64]{0,1:T(8,128)(2,1)S(1)}, bf16[1024,64]{0,1:T(8,128)(2,1)}, u32[]{:S(2)}) copy-start(bf16[1024,64]{0,1:T(8,128)(2,1)} %param.13) | copy-start | bytes 393220
  32.5 77.5 %all-gather.2.cloned.1.call-start = ((), (), s32[]{:S(2)}) async-start(), calls=%async_computation.2 | async-start | bytes 4349952 | tf_op jit(solution)/shard_map/all_gather | solution.py:57
  79.6 116.5 %all-reduce.3.cloned.1.call-start = ((), (), s32[]{:S(2)}) async-start(), calls=%async_computation.4 | async-start | bytes 262144 | tf_op jit(solution)/shard_map/psum | solution.py:90
  112.9 132.3 %all-reduce.5.cloned.1.call-start = ((), (), s32[]{:S(2)}) async-start(), calls=%async_computation.5 | async-start | bytes 2097152 | tf_op jit(solution)/shard_map/psum | solution.py:83
  114.4 206.7 %reduce-scatter.5.cloned.1.call-start = ((), (), s32[]{:S(2)}) async-start(), calls=%async_computation.3 | async-start | bytes 589824 | tf_op jit(solution)/shard_map/reduce_scatter | solution.py:74
  114.7 6.1 %copy-start.4 = (bf16[256,7520]{1,0:T(8,128)(2,1)S(1)}, bf16[256,7520]{1,0:T(8,128)(2,1)}, u32[]{:S(2)}) copy-start(bf16[256,7520]{1,0:T(8,128)(2,1)} %all-gather.2.cloned.1.call-done) | copy-start | bytes 11550724
Sparse Core Ops, SparseCore 0:
  32.6 43.6 reduce-scatter.6
  79.7 30.2 all-gather.1
  113.8 82.3 all-reduce.2
  199.2 46.0 all-reduce.4
  249.2 71.8 reduce-scatter.4

commit v2 on v1

v2 whole, which is shorter than its diff:
```python
import jax
import jax.numpy as jnp
from jax import lax
from jax.experimental import pallas as pl
from jax.experimental.pallas import tpu as pltpu
from jax.sharding import PartitionSpec as P

ADAPTER_SCALE = 2.0
MESH = pl.DeviceIdType.MESH
F32, BF16 = jnp.float32, jnp.bfloat16
CHUNK = 512
TAIL = 128
LAG_ADD, LAG_RELAY, LAG_GRAD, LAG_FORWARD, LAG_LAST, LAG_BACK = 1, 2, 3, 4, 5, 6


class Box:
    pass


def nt(left, right):
    return lax.dot_general(left, right, (((1,), (1,)), ((), ())), preferred_element_type=F32)


def tn(left, right):
    return lax.dot_general(left, right, (((0,), (0,)), ((), ())), preferred_element_type=F32)


def body(names, nj, nh, *refs):
    r = Box()
    for name, ref in zip(names, refs):
        setattr(r, name, ref)
    hidden = nj * CHUNK
    tail = r.w_gate.shape[1] - hidden
    tau, h, dp = lax.axis_index("tensor"), lax.axis_index("head"), lax.axis_index("dp")
    x, c = tau // 2, lax.rem(tau, 2)
    step = 2 * c - 1
    xp, xm, x2 = lax.rem(x + step + 4, 4), lax.rem(x - step + 4, 4), lax.rem(x + 2, 4)
    sib = {"tensor": 2 * x + 1 - c}
    nxt, prv = {"tensor": 2 * xp + c}, {"tensor": 2 * xm + c}
    pair = {"dp": 1 - dp}

    def head_peer(k):
        return {"head": lax.rem(h + k, nh)}

    barrier = pltpu.get_barrier_semaphore()
    partners = [sib, nxt, prv, pair] + [head_peer(k) for k in range(1, nh)]
    for partner in partners:
        pl.semaphore_signal(barrier, inc=1, device_id=partner, device_id_type=MESH)

    def local(src, dst, sem):
        return pltpu.make_async_copy(src, dst, sem)

    def small_loads():
        return [
            local(r.tokens, r.tok, r.small_sem.at[0]),
            local(r.cotangent, r.cot, r.small_sem.at[1]),
            local(r.routes, r.rts, r.small_sem.at[2]),
            local(r.heads, r.hup, r.small_sem.at[3]),
            local(r.factor, r.cdf, r.small_sem.at[4]),
        ]

    def chunk_loads(j):
        cols = pl.ds(pl.multiple_of(j * CHUNK, CHUNK), CHUNK)
        return [
            local(r.w_gate.at[:, cols], r.wgu.at[j, :, pl.ds(0, CHUNK)], r.load_sem.at[j, 0]),
            local(r.w_up.at[:, cols], r.wgu.at[j, :, pl.ds(CHUNK, CHUNK)], r.load_sem.at[j, 1]),
            local(r.w_down.at[cols, :], r.wd.at[j], r.load_sem.at[j, 2]),
        ]

    def tail_loads():
        cols = pl.ds(hidden, tail)
        return [
            local(r.w_gate.at[:, cols], r.raw_g, r.small_sem.at[5]),
            local(r.w_up.at[:, cols], r.raw_u, r.small_sem.at[6]),
            local(r.w_down.at[cols, :], r.t_wd.at[pl.ds(0, tail), :], r.small_sem.at[7]),
        ]

    first = small_loads()
    first[0].start()
    for load in chunk_loads(0):
        load.start()
    for load in first[1:]:
        load.start()
    r.t_wg[...] = jnp.zeros_like(r.t_wg)
    r.t_wu[...] = jnp.zeros_like(r.t_wu)
    r.t_wd[...] = jnp.zeros_like(r.t_wd)
    for load in tail_loads():
        load.start()

    def start_chunk(j, carry):
        for load in chunk_loads(j):
            load.start()
        return carry

    lax.fori_loop(1, nj, start_chunk, 0)

    def main():
        b = Box()
        b.part, b.sibs = r.m_part, r.m_sibs
        b.s1, b.s2, b.s3, b.r1, b.r2, b.r3 = r.m_s1, r.m_s2, r.m_s3, r.m_r1, r.m_r2, r.m_r3
        b.grads, b.send, b.recv, b.width = r.m_grads, r.m_send, r.m_recv, CHUNK
        return b

    def special():
        b = Box()
        b.part, b.sibs = r.t_part, r.t_sibs
        b.s1, b.s2, b.s3, b.r1, b.r2, b.r3 = r.t_s1, r.t_s2, r.t_s3, r.t_r1, r.t_r2, r.t_r3
        b.grads, b.send, b.recv, b.width = r.t_grads, r.t_send, r.t_recv, TAIL
        return b

    main, special = main(), special()

    def remote(b, j, i, src, dst, to):
        return pltpu.make_async_remote_copy(
            src_ref=src,
            dst_ref=dst,
            send_sem=b.send.at[j, i],
            recv_sem=b.recv.at[j, i],
            device_id=to,
            device_id_type=MESH,
        )

    def to_sib(b, j):
        return remote(b, j, 0, b.part.at[j, 1 - c], b.sibs.at[j], sib)

    def sum_far(b, j):
        return remote(b, j, 1, b.s1.at[j], b.r1.at[j], nxt)

    def sum_near(b, j):
        return remote(b, j, 2, b.s2.at[j], b.r2.at[j], prv)

    def sum_on(b, j):
        return remote(b, j, 3, b.s3.at[j], b.r3.at[j], nxt)

    def grad(b, j, i, slot, to):
        return remote(b, j, i, b.grads.at[j, slot], b.grads.at[j, slot], to)

    own, far, near, ahead = 2 * x + c, 2 * x2 + c, 2 * xm + c, 2 * xp + c
    sib_own, sib_far, sib_near, sib_ahead = (
        2 * x + 1 - c,
        2 * x2 + 1 - c,
        2 * xm + 1 - c,
        2 * xp + 1 - c,
    )

    def add(b, j):
        to_sib(b, j).wait_recv()
        b.s1[j] = (b.part[j, c, x2].astype(F32) + b.sibs[j, x2].astype(F32)).astype(BF16)
        sum_far(b, j).start()
        b.s2[j] = (b.part[j, c, xm].astype(F32) + b.sibs[j, xm].astype(F32)).astype(BF16)
        sum_near(b, j).start()

    def relay(b, j):
        sum_far(b, j).wait_recv()
        b.s3[j] = (
            b.r1[j].astype(F32) + b.part[j, c, xp].astype(F32) + b.sibs[j, xp].astype(F32)
        ).astype(BF16)
        sum_on(b, j).start()

    def totals(b, j):
        sum_near(b, j).wait_recv()
        sum_on(b, j).wait_recv()
        width = b.width

        def part(lo, size):
            at = pl.ds(lo, size)
            return (
                b.r3[j, :, at].astype(F32)
                + b.r2[j, :, at].astype(F32)
                + b.part[j, c, x, :, at].astype(F32)
                + b.sibs[j, x, :, at].astype(F32)
            )

        gate, up, back = (part(i * width, width) for i in range(3))
        sig = jax.nn.sigmoid(gate)
        b.grads[j, own, :, pl.ds(0, width)] = (
            back * up * sig * (1.0 + gate * (1.0 - sig))
        ).astype(BF16)
        b.grads[j, own, :, pl.ds(width, width)] = (back * gate * sig).astype(BF16)
        return part

    def spread(b, j):
        grad(b, j, 4, own, nxt).start()
        grad(b, j, 5, own, prv).start()
        grad(b, j, 6, own, sib).start()

    def forward(b, j):
        grad(b, j, 4, near, nxt).wait_recv()
        grad(b, j, 7, near, nxt).start()
        grad(b, j, 8, near, sib).start()
        grad(b, j, 5, ahead, prv).wait_recv()
        grad(b, j, 9, ahead, sib).start()

    def last(b, j):
        grad(b, j, 7, far, nxt).wait_recv()
        grad(b, j, 10, far, sib).start()

    def arrived(b, j):
        grad(b, j, 6, sib_own, sib).wait_recv()
        grad(b, j, 8, sib_ahead, sib).wait_recv()
        grad(b, j, 9, sib_near, sib).wait_recv()
        grad(b, j, 10, sib_far, sib).wait_recv()

    def all_sent(b, j):
        for copy in (to_sib(b, j), sum_far(b, j), sum_near(b, j), sum_on(b, j)):
            copy.wait_send()
        grad(b, j, 4, own, nxt).wait_send()
        grad(b, j, 5, own, prv).wait_send()
        grad(b, j, 6, own, sib).wait_send()
        grad(b, j, 7, near, nxt).wait_send()
        grad(b, j, 8, near, sib).wait_send()
        grad(b, j, 9, ahead, sib).wait_send()
        grad(b, j, 10, far, sib).wait_send()

    def store_part(b, j, lo, value):
        for q in range(4):
            for core in range(2):
                at = (2 * q + core) * 32
                b.part[j, core, q, :, pl.ds(lo, value.shape[1])] = value[at : at + 32].astype(BF16)

    def other(i, src, dst, to):
        return pltpu.make_async_remote_copy(
            src_ref=src,
            dst_ref=dst,
            send_sem=r.o_send.at[i],
            recv_sem=r.o_recv.at[i],
            device_id=to,
            device_id_type=MESH,
        )

    def pair_cot():
        return other(0, r.cot, r.p_cot, pair)

    def pair_routes():
        return other(1, r.rb, r.p_rb, pair)

    def pair_codes():
        return other(2, r.codes, r.p_codes, pair)

    def pair_shared():
        return other(3, r.shared, r.p_shared, pair)

    def code_copy(k):
        return other(4 + k, r.mine, r.hx.at[k], head_peer(k))

    def x_copy(k):
        return other(4 + nh + k, r.xs.at[k], r.xr.at[k], head_peer(k))

    first_head = h * r.hup.shape[0]
    rank = r.cdf.shape[1]

    def lanes(shape):
        return lax.broadcasted_iota(jnp.int32, shape, 1)

    def special_matmuls():
        for load in small_loads()[2:] + tail_loads():
            load.wait()
        r.t_wg[:, pl.ds(0, tail)] = r.raw_g[...]
        r.t_wu[:, pl.ds(0, tail)] = r.raw_u[...]
        r.cdf2[...] = jnp.zeros_like(r.cdf2)
        r.cdf2[:, pl.ds(rank, rank)] = r.cdf[...]
        tok, cot = r.tok[...], r.cot[...]
        store_part(special, 0, 0, jnp.dot(tok, r.t_wg[...], preferred_element_type=F32))
        store_part(special, 0, TAIL, jnp.dot(tok, r.t_wu[...], preferred_element_type=F32))
        store_part(special, 0, 2 * TAIL, nt(cot, r.t_wd[...]))
        codes = jnp.dot(tok, r.cdf2[...], preferred_element_type=F32)
        routes = r.rts[...]
        r.rb[...] = jnp.broadcast_to(routes.astype(F32), r.rb.shape).astype(BF16)
        pair_routes().start()
        total = jnp.zeros_like(codes)
        half = (lanes(codes.shape) >= rank).astype(jnp.int32)
        for p in range(r.hup.shape[0] // 2):
            flat = jnp.concatenate([r.hup[2 * p], r.hup[2 * p + 1]], axis=0)
            total += jnp.where(routes == first_head + 2 * p + half, nt(cot, flat), 0.0)
        total = ADAPTER_SCALE * (total + pltpu.roll(total, rank, 1))
        store_part(special, 0, 3 * TAIL, jnp.where(half == 0, total, codes))

    def special_totals():
        part = totals(special, 0)
        r.mine[...] = part(3 * TAIL, TAIL).astype(BF16)
        for k in range(1, nh):
            code_copy(k).start()

    def special_spread():
        mine = r.mine[...].astype(F32)
        total = mine
        for k in range(1, nh):
            code_copy(k).wait_recv()
            total += r.hx[k].astype(F32)
        total = jnp.where(lanes(mine.shape) < rank, total, mine)
        special.grads[0, own, :, pl.ds(2 * TAIL, TAIL)] = total.astype(BF16)
        spread(special, 0)

    def up_heads(codes, routes, cot, fresh):
        both = jnp.where(
            lanes(codes.shape) < rank, pltpu.roll(codes.astype(F32), rank, 1), codes.astype(F32)
        )
        half = (lanes(codes.shape) >= rank).astype(F32)
        base = first_head.astype(F32) + half
        for p in range(r.hup.shape[0] // 2):
            chosen = jnp.where(routes.astype(F32) == base + 2.0 * p, both, 0.0).astype(BF16)
            grads = (ADAPTER_SCALE * tn(chosen, cot)).reshape(2, rank, cot.shape[1])
            if fresh:
                r.uph[pl.ds(2 * p, 2)] = grads
            else:
                r.o_heads[pl.ds(2 * p, 2)] = r.uph[pl.ds(2 * p, 2)] + grads

    def special_back():
        arrived(special, 0)
        grads = special.grads[0, :, :, pl.ds(0, 2 * TAIL)].reshape(256, 2 * TAIL)
        r.acc[...] = nt(grads[:, :TAIL], r.t_wg[...]) + nt(grads[:, TAIL:], r.t_wu[...])
        codes = special.grads[0, :, :, pl.ds(2 * TAIL, TAIL)].reshape(256, TAIL)
        r.codes[...] = codes
        pair_codes().start()
        r.shared[...] = tn(r.tok[...], codes)[:, :rank].astype(BF16)
        pair_shared().start()
        up_heads(codes, r.rb[...], r.cot[...], True)
        mine = special.grads[0, h, :, pl.ds(2 * TAIL, TAIL)]
        weights = jnp.where(lanes(r.cdf2.shape) < rank, pltpu.roll(r.cdf2[...].astype(F32), rank, 1), 0.0)
        r.xcode[...] = nt(mine, weights.astype(BF16))

    def special_pair():
        pair_cot().wait_recv()
        pair_routes().wait_recv()
        pair_codes().wait_recv()
        up_heads(r.p_codes[...], r.p_rb[...], r.p_cot[...], False)
        pair_shared().wait_recv()
        r.o_shared[...] = r.shared[...].astype(F32) + r.p_shared[...].astype(F32)

    def matmuls(j):
        loads = chunk_loads(j)
        loads[0].wait()
        tok = r.tok[...]
        store_part(main, j, 0, jnp.dot(tok, r.wgu[j, :, pl.ds(0, CHUNK)], preferred_element_type=F32))
        loads[1].wait()
        store_part(
            main, j, CHUNK, jnp.dot(tok, r.wgu[j, :, pl.ds(CHUNK, CHUNK)], preferred_element_type=F32)
        )
        loads[2].wait()
        store_part(main, j, 2 * CHUNK, nt(r.cot[...], r.wd[j]))

    def back(j):
        arrived(main, j)
        grads = main.grads[j].reshape(256, 2 * CHUNK)
        for n in range(2):
            at = pl.ds(n * 512, 512)
            r.acc[:, at] += nt(grads, r.wgu[j, at, :])

    for load in small_loads()[:2]:
        load.wait()
    pl.semaphore_wait(barrier, len(partners))
    pair_cot().start()

    def tick(t, carry):
        def stage(lag, run):
            @pl.when((t >= lag) & (t < nj + lag))
            def _():
                run(t - lag)

        def once(at, run):
            pl.when(t == at)(run)

        def matmul_stage(j):
            matmuls(j)
            to_sib(main, j).start()

        def special_matmul_stage():
            special_matmuls()
            to_sib(special, 0).start()

        def grad_stage(j):
            totals(main, j)
            spread(main, j)

        stage(0, matmul_stage)
        once(0, special_matmul_stage)
        stage(LAG_ADD, lambda j: add(main, j))
        once(LAG_ADD, lambda: add(special, 0))
        stage(LAG_RELAY, lambda j: relay(main, j))
        once(LAG_RELAY, lambda: relay(special, 0))
        stage(LAG_GRAD, grad_stage)
        once(LAG_GRAD, special_totals)
        once(LAG_GRAD + 1, special_spread)
        stage(LAG_FORWARD, lambda j: forward(main, j))
        once(LAG_FORWARD + 1, lambda: forward(special, 0))
        stage(LAG_LAST, lambda j: last(main, j))
        once(LAG_LAST + 1, lambda: last(special, 0))
        once(LAG_BACK, special_back)
        stage(LAG_BACK, back)
        once(LAG_BACK + 4, special_pair)
        return carry

    lax.fori_loop(0, nj + LAG_BACK, tick, 0)

    for k in range(1, nh):
        rows = pl.ds(pl.multiple_of(lax.rem(h + k, nh) * 32, 32), 32)
        r.xs[k] = r.acc[rows, :].astype(BF16)
        x_copy(k).start()
    total = r.acc[pl.ds(pl.multiple_of(h * 32, 32), 32), :] + r.xcode[...]
    for k in range(1, nh):
        x_copy(k).wait_recv()
        total += r.xr[k].astype(F32)
    r.o_x[...] = total.astype(BF16)

    def sent(j, carry):
        all_sent(main, j)
        return carry

    lax.fori_loop(0, nj, sent, 0)
    all_sent(special, 0)
    for copy in (pair_cot(), pair_routes(), pair_codes(), pair_shared()):
        copy.wait_send()
    for k in range(1, nh):
        code_copy(k).wait_send()
        x_copy(k).wait_send()


def solution(mesh):
    nh = mesh.shape["head"]

    def step(tokens, cotangent, w_gate, w_up, w_down, factor, heads, routes):
        rows, width = tokens.shape
        nj = w_gate.shape[1] // CHUNK
        rank, count = factor.shape[1], heads.shape[0]
        shapes = {}

        def vmem(name, shape, dtype=BF16):
            shapes[name] = pltpu.VMEM(shape, dtype)

        vmem("tok", (rows, width))
        vmem("cot", (rows, width))
        vmem("p_cot", (rows, width))
        vmem("rts", (rows, 1), jnp.int32)
        vmem("hup", (count, rank, width))
        vmem("cdf", (width, rank))
        vmem("cdf2", (width, 2 * rank))
        vmem("wgu", (nj, width, 2 * CHUNK))
        vmem("wd", (nj, CHUNK, width))
        vmem("t_wg", (width, TAIL))
        vmem("t_wu", (width, TAIL))
        vmem("t_wd", (TAIL, width))
        vmem("raw_g", (width, w_gate.shape[1] - nj * CHUNK))
        vmem("raw_u", (width, w_gate.shape[1] - nj * CHUNK))
        for kind, n, unit, extra in (("m", nj, CHUNK, 0), ("t", 1, TAIL, TAIL)):
            full = 3 * unit + extra
            vmem(kind + "_part", (n, 2, 4, 32, full))
            vmem(kind + "_sibs", (n, 4, 32, full))
            for name in ("s1", "s2", "s3", "r1", "r2", "r3"):
                vmem(kind + "_" + name, (n, 32, full))
            vmem(kind + "_grads", (n, 8, 32, 2 * unit + extra))
            shapes[kind + "_send"] = pltpu.SemaphoreType.DMA((n, 11))
            shapes[kind + "_recv"] = pltpu.SemaphoreType.DMA((n, 11))
        vmem("rb", (rows, 2 * rank))
        vmem("p_rb", (rows, 2 * rank))
        vmem("codes", (rows, 2 * rank))
        vmem("p_codes", (rows, 2 * rank))
        vmem("shared", (width, rank))
        vmem("p_shared", (width, rank))
        vmem("mine", (32, 2 * rank))
        vmem("hx", (nh, 32, 2 * rank))
        vmem("xs", (nh, 32, width))
        vmem("xr", (nh, 32, width))
        vmem("acc", (rows, width), F32)
        vmem("xcode", (32, width), F32)
        vmem("uph", (count, rank, width), F32)
        shapes["o_send"] = pltpu.SemaphoreType.DMA((4 + 2 * nh,))
        shapes["o_recv"] = pltpu.SemaphoreType.DMA((4 + 2 * nh,))
        shapes["small_sem"] = pltpu.SemaphoreType.DMA((8,))
        shapes["load_sem"] = pltpu.SemaphoreType.DMA((nj, 3))
        names = ["tokens", "cotangent", "w_gate", "w_up", "w_down", "factor", "heads", "routes"]
        names += ["o_x", "o_shared", "o_heads"] + list(shapes)

        def kernel(*refs):
            body(names, nj, nh, *refs)

        any_space = pl.BlockSpec(memory_space=pl.ANY)
        return pl.pallas_call(
            kernel,
            out_shape=(
                jax.ShapeDtypeStruct((32, width), BF16),
                jax.ShapeDtypeStruct((width, rank), F32),
                jax.ShapeDtypeStruct((count, rank, width), F32),
            ),
            in_specs=[any_space] * 8,
            out_specs=(pl.BlockSpec(memory_space=pltpu.VMEM),) * 3,
            scratch_shapes=list(shapes.values()),
            compiler_params=pltpu.CompilerParams(
                collective_id=0, has_side_effects=True, vmem_limit_bytes=60 * 1024 * 1024
            ),
            name="ffn_backward",
        )(tokens, cotangent, w_gate, w_up, w_down, factor, heads, routes)

    placed = (
        P("dp", "tensor"),
        P("dp", "tensor"),
        P("tensor", "head"),
        P("tensor", "head"),
        P("head", "tensor"),
        P("tensor", None),
        P("head", None, "tensor"),
        P("dp", None),
    )
    return jax.shard_map(
        step,
        mesh=mesh,
        in_specs=placed,
        out_specs=(P(("dp", "head"), "tensor"), P("tensor", None), P("head", None, "tensor")),
        check_vma=False,
    )
```

time: 328 us -> 101 us (0.31)
  waiting for transfers between devices: 263 us -> 0 us
  Pallas kernels: 0 us -> 69.1 us
  matrix products: 31.2 us -> 0 us
  local copies, waits for them, and re-layouts: 11.4 us -> 30.2 us
  between operations: 13.9 us -> 0.64 us
  other arithmetic: 7.4 us -> 0 us
    reduce_scatter x2 -> x0, waiting for transfers between devices: 117 us -> none  [the longest x1 73.1 us: local(): lax.psum_scatter(ffn_part.astype(jnp.bfloat16), 'head', scatter_dimension...]
    psum x2 -> x0, waiting for transfers between devices: 116 us -> none  [the longest x1 68.6 us: local(): lax.psum(shared_term.astype(jnp.bfloat16), ('dp', 'head'))]
    pallas_call x0 -> x1, Pallas kernels: none -> 69.1 us  [step(): pl.pallas_call(kernel, out_shape=(jax.ShapeDtypeStruct((32, width), BF16)...]
    dot_general x10 -> x0, matrix products: 31.2 us -> none  [the longest x5 16.7 us: contract_last(): lax.dot_general(left, right, (((1,), (1,)), ((), ())), preferred_element_...]
    all_gather x1 -> x0, waiting for transfers between devices: 30.3 us -> none  [local(): lax.all_gather(jnp.concatenate([gate_gradient, up_gradient, own_rows[:, 3...]
    unnamed x17 -> x6, local copies, waits for them, and re-layouts: 8.5 us -> 28.3 us
    convert_element_type x4 -> x0, other arithmetic: 6.76 us -> none  [the longest x1 2.79 us: local(): up_head_gradients = lax.psum(head_contributions.reshape(local_heads, redu...]
  transfers between devices with their start and end apart: 5 -> 0, of which waited for: 5 -> 0; matrix products, arithmetic and copies ran while one was open for 6% -> 0% of each run, Pallas kernels for 0% -> 0%
where the time goes in v2:
time: 101 us; the launch traced here: 100 us
  Pallas kernels  69.1 us (68%)
  local copies, waits for them, and re-layouts  30.2 us (30%)
    pallas_call x1, Pallas kernels, step(): pl.pallas_call(kernel, out_shape=(jax.ShapeDtypeStruct((32, width), BF16)...  69.1 us
    unnamed x6, local copies, waits for them, and re-layouts  28.3 us

profile of v2, /device:TPU:0, one launch (start us, length us, event | category | flops | bytes accessed | tf_op | source)
XLA Modules:
  0.0 100.0 jit_solution(11806657306624836731)
XLA Ops:
  0.6 1.5 %copy.14.refs_7_ = s32[256,1]{1,0:T(8,128)} copy(s32[256,1]{0,1:T(1,128)} %param.15) | data formatting | bytes 2048 | tf_op args[7]
  2.1 1.7 %copy.13.refs_5_ = bf16[1024,64]{1,0:T(8,128)(2,1)} copy(bf16[1024,64]{0,1:T(8,128)(2,1)} %param.13) | data formatting | bytes 262144 | tf_op args[5]
  3.8 10.2 %copy.11.refs_2_ = bf16[1024,3696]{1,0:T(8,128)(2,1)} copy(bf16[1024,3696]{0,1:T(8,128)(2,1)} %param.10) | data formatting | bytes 15138816 | tf_op args[2]
  14.0 10.3 %copy.12.refs_3_ = bf16[1024,3696]{1,0:T(8,128)(2,1)} copy(bf16[1024,3696]{0,1:T(8,128)(2,1)} %param.11) | data formatting | bytes 15138816 | tf_op args[3]
  24.3 69.1 %ffn_backward.1 = (bf16[32,1024]{1,0:T(8,128)(2,1)}, f32[1024,64]{1,0:T(8,128)}, f32[8,64,1024]{2,1,0:T(8,128)}) custom-call(bf16[256,1024]{1,0:T(8,128)(2,1)} %refs_0_.1, bf16[256,1024]{1,0:T(8,128)(2,1)} %refs_1_.1, bf16[1024,3696]{1,0:T(8,128)(2,1)} %copy.11.refs_2_, bf16[1024,3696]{1,0:T(8,128)(2,1)} %copy.12.refs_3_, bf16[3696,1024]{1,0:T(8,128)(2,1)} %refs_4_.1, ...), custom_call_target="tpu_custom_call" | custom-call | tf_op jit(solution)/shard_map/ffn_backward/pallas_call | solution.py:477
  93.5 1.9 %copy.15 = f32[1024,64]{0,1:T(8,128)} copy(f32[1024,64]{1,0:T(8,128)} %get-tuple-element.4) | data formatting | bytes 524288 | tf_op jit(solution)/shard_map/ffn_backward/pallas_call | solution.py:477
  95.4 1.5 %copy.18 = bf16[32,1024]{1,0:T(8,128)(2,1)} copy(bf16[32,1024]{1,0:T(8,128)(2,1)} %get-tuple-element.9) | data formatting | bytes 131072
  96.9 3.2 %copy.19 = f32[8,64,1024]{2,1,0:T(8,128)} copy(f32[8,64,1024]{2,1,0:T(8,128)} %get-tuple-element.11) | data formatting | bytes 4194304

commit v3 on v2

--- a/solution.py
+++ b/solution.py
@@ -30,7 +30,7 @@
     for name, ref in zip(names, refs):
         setattr(r, name, ref)
     hidden = nj * CHUNK
-    tail = r.w_gate.shape[1] - hidden
+    tail = r.w_gate.shape[0] - hidden
     tau, h, dp = lax.axis_index("tensor"), lax.axis_index("head"), lax.axis_index("dp")
     x, c = tau // 2, lax.rem(tau, 2)
     step = 2 * c - 1
@@ -60,19 +60,19 @@
         ]
 
     def chunk_loads(j):
-        cols = pl.ds(pl.multiple_of(j * CHUNK, CHUNK), CHUNK)
+        rows = pl.ds(pl.multiple_of(j * CHUNK, CHUNK), CHUNK)
         return [
-            local(r.w_gate.at[:, cols], r.wgu.at[j, :, pl.ds(0, CHUNK)], r.load_sem.at[j, 0]),
-            local(r.w_up.at[:, cols], r.wgu.at[j, :, pl.ds(CHUNK, CHUNK)], r.load_sem.at[j, 1]),
-            local(r.w_down.at[cols, :], r.wd.at[j], r.load_sem.at[j, 2]),
+            local(r.w_gate.at[rows, :], r.wgu.at[j, pl.ds(0, CHUNK), :], r.load_sem.at[j, 0]),
+            local(r.w_up.at[rows, :], r.wgu.at[j, pl.ds(CHUNK, CHUNK), :], r.load_sem.at[j, 1]),
+            local(r.w_down.at[rows, :], r.wd.at[j], r.load_sem.at[j, 2]),
         ]
 
     def tail_loads():
-        cols = pl.ds(hidden, tail)
+        rows = pl.ds(hidden, tail)
         return [
-            local(r.w_gate.at[:, cols], r.raw_g, r.small_sem.at[5]),
-            local(r.w_up.at[:, cols], r.raw_u, r.small_sem.at[6]),
-            local(r.w_down.at[cols, :], r.t_wd.at[pl.ds(0, tail), :], r.small_sem.at[7]),
+            local(r.w_gate.at[rows, :], r.t_wgu.at[pl.ds(0, tail), :], r.small_sem.at[5]),
+            local(r.w_up.at[rows, :], r.t_wgu.at[pl.ds(TAIL, tail), :], r.small_sem.at[6]),
+            local(r.w_down.at[rows, :], r.t_wd.at[pl.ds(0, tail), :], r.small_sem.at[7]),
         ]
 
     first = small_loads()
@@ -81,8 +81,7 @@
         load.start()
     for load in first[1:]:
         load.start()
-    r.t_wg[...] = jnp.zeros_like(r.t_wg)
-    r.t_wu[...] = jnp.zeros_like(r.t_wu)
+    r.t_wgu[...] = jnp.zeros_like(r.t_wgu)
     r.t_wd[...] = jnp.zeros_like(r.t_wd)
     for load in tail_loads():
         load.start()
@@ -247,7 +246,7 @@
         return other(4 + nh + k, r.xs.at[k], r.xr.at[k], head_peer(k))
 
     first_head = h * r.hup.shape[0]
-    rank = r.cdf.shape[1]
+    rank = r.cdf.shape[0]
 
     def lanes(shape):
         return lax.broadcasted_iota(jnp.int32, shape, 1)
@@ -255,25 +254,24 @@
     def special_matmuls():
         for load in small_loads()[2:] + tail_loads():
             load.wait()
-        r.t_wg[:, pl.ds(0, tail)] = r.raw_g[...]
-        r.t_wu[:, pl.ds(0, tail)] = r.raw_u[...]
-        r.cdf2[...] = jnp.zeros_like(r.cdf2)
-        r.cdf2[:, pl.ds(rank, rank)] = r.cdf[...]
+        factor = r.cdf[...]
+        upper = jnp.concatenate([jnp.zeros_like(factor), factor], axis=0)
         tok, cot = r.tok[...], r.cot[...]
-        store_part(special, 0, 0, jnp.dot(tok, r.t_wg[...], preferred_element_type=F32))
-        store_part(special, 0, TAIL, jnp.dot(tok, r.t_wu[...], preferred_element_type=F32))
+        store_part(special, 0, 0, nt(tok, r.t_wgu[...]))
         store_part(special, 0, 2 * TAIL, nt(cot, r.t_wd[...]))
-        codes = jnp.dot(tok, r.cdf2[...], preferred_element_type=F32)
-        routes = r.rts[...]
-        r.rb[...] = jnp.broadcast_to(routes.astype(F32), r.rb.shape).astype(BF16)
+        codes = nt(tok, upper)
+        row = r.rts[...].astype(F32)
+        routes = jnp.broadcast_to(row, (2 * rank, row.shape[1])).T
+        r.rb[...] = routes.astype(BF16)
         pair_routes().start()
         total = jnp.zeros_like(codes)
-        half = (lanes(codes.shape) >= rank).astype(jnp.int32)
+        half = (lanes(codes.shape) >= rank).astype(F32)
+        base = first_head.astype(F32) + half
         for p in range(r.hup.shape[0] // 2):
             flat = jnp.concatenate([r.hup[2 * p], r.hup[2 * p + 1]], axis=0)
-            total += jnp.where(routes == first_head + 2 * p + half, nt(cot, flat), 0.0)
+            total += jnp.where(routes == base + 2.0 * p, nt(cot, flat), 0.0)
         total = ADAPTER_SCALE * (total + pltpu.roll(total, rank, 1))
-        store_part(special, 0, 3 * TAIL, jnp.where(half == 0, total, codes))
+        store_part(special, 0, 3 * TAIL, jnp.where(half == 0.0, total, codes))
 
     def special_totals():
         part = totals(special, 0)
@@ -290,6 +288,10 @@
         total = jnp.where(lanes(mine.shape) < rank, total, mine)
         special.grads[0, own, :, pl.ds(2 * TAIL, TAIL)] = total.astype(BF16)
         spread(special, 0)
+
+    def heads_out(p):
+        at = pl.ds(2 * p, 2)
+        return local(r.uph.at[at], r.o_heads.at[at], r.out_sem.at[p])
 
     def up_heads(codes, routes, cot, fresh):
         both = jnp.where(
@@ -303,21 +305,23 @@
             if fresh:
                 r.uph[pl.ds(2 * p, 2)] = grads
             else:
-                r.o_heads[pl.ds(2 * p, 2)] = r.uph[pl.ds(2 * p, 2)] + grads
+                r.uph[pl.ds(2 * p, 2)] += grads
+                heads_out(p).start()
 
     def special_back():
         arrived(special, 0)
         grads = special.grads[0, :, :, pl.ds(0, 2 * TAIL)].reshape(256, 2 * TAIL)
-        r.acc[...] = nt(grads[:, :TAIL], r.t_wg[...]) + nt(grads[:, TAIL:], r.t_wu[...])
+        r.acc[...] = jnp.dot(grads, r.t_wgu[...], preferred_element_type=F32)
         codes = special.grads[0, :, :, pl.ds(2 * TAIL, TAIL)].reshape(256, TAIL)
         r.codes[...] = codes
         pair_codes().start()
-        r.shared[...] = tn(r.tok[...], codes)[:, :rank].astype(BF16)
+        r.shared[...] = tn(codes, r.tok[...])[:rank].astype(BF16)
         pair_shared().start()
         up_heads(codes, r.rb[...], r.cot[...], True)
         mine = special.grads[0, h, :, pl.ds(2 * TAIL, TAIL)]
-        weights = jnp.where(lanes(r.cdf2.shape) < rank, pltpu.roll(r.cdf2[...].astype(F32), rank, 1), 0.0)
-        r.xcode[...] = nt(mine, weights.astype(BF16))
+        factor = r.cdf[...]
+        lower = jnp.concatenate([factor, jnp.zeros_like(factor)], axis=0)
+        r.xcode[...] = jnp.dot(mine, lower, preferred_element_type=F32)
 
     def special_pair():
         pair_cot().wait_recv()
@@ -331,11 +335,9 @@
         loads = chunk_loads(j)
         loads[0].wait()
         tok = r.tok[...]
-        store_part(main, j, 0, jnp.dot(tok, r.wgu[j, :, pl.ds(0, CHUNK)], preferred_element_type=F32))
+        store_part(main, j, 0, nt(tok, r.wgu[j, pl.ds(0, CHUNK), :]))
         loads[1].wait()
-        store_part(
-            main, j, CHUNK, jnp.dot(tok, r.wgu[j, :, pl.ds(CHUNK, CHUNK)], preferred_element_type=F32)
-        )
+        store_part(main, j, CHUNK, nt(tok, r.wgu[j, pl.ds(CHUNK, CHUNK), :]))
         loads[2].wait()
         store_part(main, j, 2 * CHUNK, nt(r.cot[...], r.wd[j]))
 
@@ -344,7 +346,7 @@
         grads = main.grads[j].reshape(256, 2 * CHUNK)
         for n in range(2):
             at = pl.ds(n * 512, 512)
-            r.acc[:, at] += nt(grads, r.wgu[j, at, :])
+            r.acc[:, at] += jnp.dot(grads, r.wgu[j, :, at], preferred_element_type=F32)
 
     for load in small_loads()[:2]:
         load.wait()
@@ -408,6 +410,8 @@
 
     lax.fori_loop(0, nj, sent, 0)
     all_sent(special, 0)
+    for p in range(r.hup.shape[0] // 2):
+        heads_out(p).wait()
     for copy in (pair_cot(), pair_routes(), pair_codes(), pair_shared()):
         copy.wait_send()
     for k in range(1, nh):
@@ -415,13 +419,27 @@
         x_copy(k).wait_send()
 
 
+def finish(x_in, shared_in, heads_in, x_out, shared_out, heads_out, sems):
+    count = heads_in.shape[0]
+    copies = [
+        pltpu.make_async_copy(heads_in.at[e], heads_out.at[e], sems.at[e]) for e in range(count)
+    ]
+    copies.append(pltpu.make_async_copy(x_in, x_out, sems.at[count]))
+    copies.append(pltpu.make_async_copy(shared_in, shared_out, sems.at[count + 1]))
+    for copy in copies:
+        copy.start()
+    for copy in copies:
+        copy.wait()
+
+
 def solution(mesh):
     nh = mesh.shape["head"]
 
     def step(tokens, cotangent, w_gate, w_up, w_down, factor, heads, routes):
         rows, width = tokens.shape
-        nj = w_gate.shape[1] // CHUNK
-        rank, count = factor.shape[1], heads.shape[0]
+        w_gate, w_up, factor, routes = w_gate.T, w_up.T, factor.T, routes.T
+        nj = w_gate.shape[0] // CHUNK
+        rank, count = factor.shape[0], heads.shape[0]
         shapes = {}
 
         def vmem(name, shape, dtype=BF16):
@@ -430,17 +448,13 @@
         vmem("tok", (rows, width))
         vmem("cot", (rows, width))
         vmem("p_cot", (rows, width))
-        vmem("rts", (rows, 1), jnp.int32)
+        vmem("rts", (1, rows), jnp.int32)
         vmem("hup", (count, rank, width))
-        vmem("cdf", (width, rank))
-        vmem("cdf2", (width, 2 * rank))
-        vmem("wgu", (nj, width, 2 * CHUNK))
+        vmem("cdf", (rank, width))
+        vmem("wgu", (nj, 2 * CHUNK, width))
         vmem("wd", (nj, CHUNK, width))
-        vmem("t_wg", (width, TAIL))
-        vmem("t_wu", (width, TAIL))
+        vmem("t_wgu", (2 * TAIL, width))
         vmem("t_wd", (TAIL, width))
-        vmem("raw_g", (width, w_gate.shape[1] - nj * CHUNK))
-        vmem("raw_u", (width, w_gate.shape[1] - nj * CHUNK))
         for kind, n, unit, extra in (("m", nj, CHUNK, 0), ("t", 1, TAIL, TAIL)):
             full = 3 * unit + extra
             vmem(kind + "_part", (n, 2, 4, 32, full))
@@ -454,8 +468,8 @@
         vmem("p_rb", (rows, 2 * rank))
         vmem("codes", (rows, 2 * rank))
         vmem("p_codes", (rows, 2 * rank))
-        vmem("shared", (width, rank))
-        vmem("p_shared", (width, rank))
+        vmem("shared", (rank, width))
+        vmem("p_shared", (rank, width))
         vmem("mine", (32, 2 * rank))
         vmem("hx", (nh, 32, 2 * rank))
         vmem("xs", (nh, 32, width))
@@ -465,6 +479,7 @@
         vmem("uph", (count, rank, width), F32)
         shapes["o_send"] = pltpu.SemaphoreType.DMA((4 + 2 * nh,))
         shapes["o_recv"] = pltpu.SemaphoreType.DMA((4 + 2 * nh,))
+        shapes["out_sem"] = pltpu.SemaphoreType.DMA((count // 2,))
         shapes["small_sem"] = pltpu.SemaphoreType.DMA((8,))
         shapes["load_sem"] = pltpu.SemaphoreType.DMA((nj, 3))
         names = ["tokens", "cotangent", "w_gate", "w_up", "w_down", "factor", "heads", "routes"]
@@ -474,21 +489,34 @@
             body(names, nj, nh, *refs)
 
         any_space = pl.BlockSpec(memory_space=pl.ANY)
-        return pl.pallas_call(
+        made = pl.pallas_call(
             kernel,
             out_shape=(
                 jax.ShapeDtypeStruct((32, width), BF16),
-                jax.ShapeDtypeStruct((width, rank), F32),
+                jax.ShapeDtypeStruct((rank, width), F32),
                 jax.ShapeDtypeStruct((count, rank, width), F32),
             ),
             in_specs=[any_space] * 8,
-            out_specs=(pl.BlockSpec(memory_space=pltpu.VMEM),) * 3,
+            out_specs=(
+                pl.BlockSpec(memory_space=pltpu.VMEM),
+                pl.BlockSpec(memory_space=pltpu.VMEM),
+                any_space,
+            ),
             scratch_shapes=list(shapes.values()),
             compiler_params=pltpu.CompilerParams(
                 collective_id=0, has_side_effects=True, vmem_limit_bytes=60 * 1024 * 1024
             ),
             name="ffn_backward",
         )(tokens, cotangent, w_gate, w_up, w_down, factor, heads, routes)
+        grad_x, shared, up = pl.pallas_call(
+            finish,
+            out_shape=tuple(jax.ShapeDtypeStruct(m.shape, m.dtype) for m in made),
+            in_specs=[any_space] * 3,
+            out_specs=(any_space,) * 3,
+            scratch_shapes=[pltpu.SemaphoreType.DMA((count + 2,))],
+            name="write_out",
+        )(*made)
+        return grad_x, shared.T, up
 
     placed = (
         P("dp", "tensor"),

time: 101 us -> 144 us (1.43)
  Pallas kernels: 69.1 us -> 143 us
  local copies, waits for them, and re-layouts: 30.2 us -> 0 us
    pallas_call x0 -> x1, Pallas kernels: none -> 74.6 us  [step(): pl.pallas_call(finish, out_shape=tuple((jax.ShapeDtypeStruct(m.shape, m.d...]
    unnamed x6 -> x0, local copies, waits for them, and re-layouts: 28.3 us -> none
    pallas_call x1 -> x0, local copies, waits for them, and re-layouts: 1.93 us -> none  [step(): pl.pallas_call(kernel, out_shape=(jax.ShapeDtypeStruct((32, width), BF16)...]
where the time goes in v3:
time: 144 us; the launch traced here: 143 us
  Pallas kernels  143 us (99%)
    pallas_call x1, Pallas kernels, step(): pl.pallas_call(finish, out_shape=tuple((jax.ShapeDtypeStruct(m.shape, m.d...  74.6 us
    pallas_call x1, Pallas kernels, step(): pl.pallas_call(kernel, out_shape=(jax.ShapeDtypeStruct((32, width), BF16)...  68 us

profile of v3, /device:TPU:0, one launch (start us, length us, event | category | flops | bytes accessed | tf_op | source)
XLA Modules:
  0.0 143.3 jit_solution(16605542914591310499)
XLA Ops:
  0.6 68.0 %ffn_backward.1 = (bf16[32,1024]{1,0:T(8,128)(2,1)}, f32[64,1024]{1,0:T(8,128)}, f32[8,64,1024]{2,1,0:T(8,128)}) custom-call(bf16[256,1024]{1,0:T(8,128)(2,1)} %refs_0_.1, bf16[256,1024]{1,0:T(8,128)(2,1)} %refs_1_.1, bf16[3696,1024]{1,0:T(8,128)(2,1)} %bitcast.5, bf16[3696,1024]{1,0:T(8,128)(2,1)} %bitcast.6, bf16[3696,1024]{1,0:T(8,128)(2,1)} %refs_4_.1, ...), custom_call_target="tpu_custom_call" | custom-call | tf_op jit(solution)/shard_map/ffn_backward/pallas_call | solution.py:492
  68.6 74.6 %write_out.1 = (bf16[32,1024]{1,0:T(8,128)(2,1)}, f32[64,1024]{1,0:T(8,128)}, f32[8,64,1024]{2,1,0:T(8,128)}) custom-call(bf16[32,1024]{1,0:T(8,128)(2,1)} %get-tuple-element.9.x_in, f32[64,1024]{1,0:T(8,128)} %get-tuple-element.10.shared_in, f32[8,64,1024]{2,1,0:T(8,128)} %get-tuple-element.11.heads_in), custom_call_target="tpu_custom_call" | custom-call | tf_op jit(solution)/shard_map/write_out/pallas_call | solution.py:511

commit v4 on v3

--- a/solution.py
+++ b/solution.py
@@ -10,7 +10,7 @@
 F32, BF16 = jnp.float32, jnp.bfloat16
 CHUNK = 512
 TAIL = 128
-LAG_ADD, LAG_RELAY, LAG_GRAD, LAG_FORWARD, LAG_LAST, LAG_BACK = 1, 2, 3, 4, 5, 6
+LAG_ADD, LAG_RELAY, LAG_GRAD, LAG_FORWARD, LAG_LAST, LAG_BACK = 1, 3, 5, 7, 9, 11
 
 
 class Box:
@@ -419,17 +419,19 @@
         x_copy(k).wait_send()
 
 
-def finish(x_in, shared_in, heads_in, x_out, shared_out, heads_out, sems):
+def finish(x_in, shared_in, heads_in, x_out, shared_out, heads_out, x, shared, heads, came, left):
     count = heads_in.shape[0]
-    copies = [
-        pltpu.make_async_copy(heads_in.at[e], heads_out.at[e], sems.at[e]) for e in range(count)
-    ]
-    copies.append(pltpu.make_async_copy(x_in, x_out, sems.at[count]))
-    copies.append(pltpu.make_async_copy(shared_in, shared_out, sems.at[count + 1]))
-    for copy in copies:
-        copy.start()
-    for copy in copies:
-        copy.wait()
+    steps = [(heads_in.at[e], heads.at[e], heads_out.at[e]) for e in range(count)]
+    steps += [(shared_in, shared, shared_out), (x_in, x, x_out)]
+    reads = [pltpu.make_async_copy(a, b, came.at[i]) for i, (a, b, _) in enumerate(steps)]
+    writes = [pltpu.make_async_copy(b, c, left.at[i]) for i, (_, b, c) in enumerate(steps)]
+    for read in reads:
+        read.start()
+    for read, write in zip(reads, writes):
+        read.wait()
+        write.start()
+    for write in writes:
+        write.wait()
 
 
 def solution(mesh):
@@ -513,7 +515,8 @@
             out_shape=tuple(jax.ShapeDtypeStruct(m.shape, m.dtype) for m in made),
             in_specs=[any_space] * 3,
             out_specs=(any_space,) * 3,
-            scratch_shapes=[pltpu.SemaphoreType.DMA((count + 2,))],
+            scratch_shapes=[pltpu.VMEM(m.shape, m.dtype) for m in made]
+            + [pltpu.SemaphoreType.DMA((count + 2,))] * 2,
             name="write_out",
         )(*made)
         return grad_x, shared.T, up

time: 144 us -> 70.5 us (0.49)
  Pallas kernels: 143 us -> 69.7 us
    pallas_call x1, Pallas kernels: 74.6 us -> 2.53 us  [step(): pl.pallas_call(finish, out_shape=tuple((jax.ShapeDtypeStruct(m.shape, m.d...]
where the time goes in v4:
time: 70.5 us; the launch traced here: 70.3 us
  Pallas kernels  69.7 us (99%)
    pallas_call x1, Pallas kernels, step(): pl.pallas_call(kernel, out_shape=(jax.ShapeDtypeStruct((32, width), BF16)...  67.2 us
    pallas_call x1, Pallas kernels, step(): pl.pallas_call(finish, out_shape=tuple((jax.ShapeDtypeStruct(m.shape, m.d...  2.53 us

profile of v4, /device:TPU:0, one launch (start us, length us, event | category | flops | bytes accessed | tf_op | source)
XLA Modules:
  0.0 70.3 jit_solution(4990850244117146921)
XLA Ops:
  0.6 67.2 %ffn_backward.1 = (bf16[32,1024]{1,0:T(8,128)(2,1)}, f32[64,1024]{1,0:T(8,128)}, f32[8,64,1024]{2,1,0:T(8,128)}) custom-call(bf16[256,1024]{1,0:T(8,128)(2,1)} %refs_0_.1, bf16[256,1024]{1,0:T(8,128)(2,1)} %refs_1_.1, bf16[3696,1024]{1,0:T(8,128)(2,1)} %bitcast.5, bf16[3696,1024]{1,0:T(8,128)(2,1)} %bitcast.6, bf16[3696,1024]{1,0:T(8,128)(2,1)} %refs_4_.1, ...), custom_call_target="tpu_custom_call" | custom-call | tf_op jit(solution)/shard_map/ffn_backward/pallas_call | solution.py:494
  67.8 2.5 %write_out.1 = (bf16[32,1024]{1,0:T(8,128)(2,1)}, f32[64,1024]{1,0:T(8,128)}, f32[8,64,1024]{2,1,0:T(8,128)}) custom-call(bf16[32,1024]{1,0:T(8,128)(2,1)} %get-tuple-element.9.x_in, f32[64,1024]{1,0:T(8,128)} %get-tuple-element.10.shared_in, f32[8,64,1024]{2,1,0:T(8,128)} %get-tuple-element.11.heads_in), custom_call_target="tpu_custom_call" | custom-call | tf_op jit(solution)/shard_map/write_out/pallas_call | solution.py:513

commit v5 on v4

--- a/solution.py
+++ b/solution.py
@@ -291,7 +291,10 @@
 
     def heads_out(p):
         at = pl.ds(2 * p, 2)
-        return local(r.uph.at[at], r.o_heads.at[at], r.out_sem.at[p])
+        return local(r.up16.at[at], r.o_heads.at[at], r.out_sem.at[p])
+
+    def shared_out():
+        return local(r.total, r.o_shared, r.out_sem.at[r.hup.shape[0] // 2])
 
     def up_heads(codes, routes, cot, fresh):
         both = jnp.where(
@@ -305,7 +308,7 @@
             if fresh:
                 r.uph[pl.ds(2 * p, 2)] = grads
             else:
-                r.uph[pl.ds(2 * p, 2)] += grads
+                r.up16[pl.ds(2 * p, 2)] = (r.uph[pl.ds(2 * p, 2)] + grads).astype(BF16)
                 heads_out(p).start()
 
     def special_back():
@@ -329,7 +332,8 @@
         pair_codes().wait_recv()
         up_heads(r.p_codes[...], r.p_rb[...], r.p_cot[...], False)
         pair_shared().wait_recv()
-        r.o_shared[...] = r.shared[...].astype(F32) + r.p_shared[...].astype(F32)
+        r.total[...] = r.shared[...].astype(F32) + r.p_shared[...].astype(F32)
+        shared_out().start()
 
     def matmuls(j):
         loads = chunk_loads(j)
@@ -412,6 +416,7 @@
     all_sent(special, 0)
     for p in range(r.hup.shape[0] // 2):
         heads_out(p).wait()
+    shared_out().wait()
     for copy in (pair_cot(), pair_routes(), pair_codes(), pair_shared()):
         copy.wait_send()
     for k in range(1, nh):
@@ -419,17 +424,31 @@
         x_copy(k).wait_send()
 
 
-def finish(x_in, shared_in, heads_in, x_out, shared_out, heads_out, x, shared, heads, came, left):
+def finish(x_in, shared_in, heads_in, x_out, shared_out, heads_out, x, shared, half, heads, came, left):
     count = heads_in.shape[0]
-    steps = [(heads_in.at[e], heads.at[e], heads_out.at[e]) for e in range(count)]
-    steps += [(shared_in, shared, shared_out), (x_in, x, x_out)]
-    reads = [pltpu.make_async_copy(a, b, came.at[i]) for i, (a, b, _) in enumerate(steps)]
-    writes = [pltpu.make_async_copy(b, c, left.at[i]) for i, (_, b, c) in enumerate(steps)]
+
+    def heads_read(e):
+        return pltpu.make_async_copy(heads_in.at[e], half.at[e], came.at[e])
+
+    def heads_write(e):
+        return pltpu.make_async_copy(heads.at[e], heads_out.at[e], left.at[e])
+
+    steps = [(shared_in, shared, shared_out), (x_in, x, x_out)]
+    reads = [pltpu.make_async_copy(a, b, came.at[count + i]) for i, (a, b, _) in enumerate(steps)]
+    writes = [pltpu.make_async_copy(b, c, left.at[count + i]) for i, (_, b, c) in enumerate(steps)]
+    for e in range(count):
+        heads_read(e).start()
     for read in reads:
         read.start()
+    for e in range(count):
+        heads_read(e).wait()
+        heads[e] = half[e].astype(F32)
+        heads_write(e).start()
     for read, write in zip(reads, writes):
         read.wait()
         write.start()
+    for e in range(count):
+        heads_write(e).wait()
     for write in writes:
         write.wait()
 
@@ -479,9 +498,11 @@
         vmem("acc", (rows, width), F32)
         vmem("xcode", (32, width), F32)
         vmem("uph", (count, rank, width), F32)
+        vmem("up16", (count, rank, width))
+        vmem("total", (rank, width), F32)
         shapes["o_send"] = pltpu.SemaphoreType.DMA((4 + 2 * nh,))
         shapes["o_recv"] = pltpu.SemaphoreType.DMA((4 + 2 * nh,))
-        shapes["out_sem"] = pltpu.SemaphoreType.DMA((count // 2,))
+        shapes["out_sem"] = pltpu.SemaphoreType.DMA((count // 2 + 1,))
         shapes["small_sem"] = pltpu.SemaphoreType.DMA((8,))
         shapes["load_sem"] = pltpu.SemaphoreType.DMA((nj, 3))
         names = ["tokens", "cotangent", "w_gate", "w_up", "w_down", "factor", "heads", "routes"]
@@ -496,12 +517,12 @@
             out_shape=(
                 jax.ShapeDtypeStruct((32, width), BF16),
                 jax.ShapeDtypeStruct((rank, width), F32),
-                jax.ShapeDtypeStruct((count, rank, width), F32),
+                jax.ShapeDtypeStruct((count, rank, width), BF16),
             ),
             in_specs=[any_space] * 8,
             out_specs=(
                 pl.BlockSpec(memory_space=pltpu.VMEM),
-                pl.BlockSpec(memory_space=pltpu.VMEM),
+                any_space,
                 any_space,
             ),
             scratch_shapes=list(shapes.values()),
@@ -512,10 +533,15 @@
         )(tokens, cotangent, w_gate, w_up, w_down, factor, heads, routes)
         grad_x, shared, up = pl.pallas_call(
             finish,
-            out_shape=tuple(jax.ShapeDtypeStruct(m.shape, m.dtype) for m in made),
+            out_shape=(
+                jax.ShapeDtypeStruct(made[0].shape, BF16),
+                jax.ShapeDtypeStruct(made[1].shape, F32),
+                jax.ShapeDtypeStruct(made[2].shape, F32),
+            ),
             in_specs=[any_space] * 3,
             out_specs=(any_space,) * 3,
             scratch_shapes=[pltpu.VMEM(m.shape, m.dtype) for m in made]
+            + [pltpu.VMEM(made[2].shape, F32)]
             + [pltpu.SemaphoreType.DMA((count + 2,))] * 2,
             name="write_out",
         )(*made)

time: 70.5 us -> 70.4 us (level)
  no operation moved by 1% of the time
where the time goes in v5:
time: 70.4 us; the launch traced here: 70.2 us
  Pallas kernels  69.5 us (99%)
    pallas_call x1, Pallas kernels, step(): pl.pallas_call(kernel, out_shape=(jax.ShapeDtypeStruct((32, width), BF16)...  67 us
    pallas_call x1, Pallas kernels, step(): pl.pallas_call(finish, out_shape=(jax.ShapeDtypeStruct(made[0].shape, BF1...  2.5 us

profile of v5, /device:TPU:0, one launch (start us, length us, event | category | flops | bytes accessed | tf_op | source)
XLA Modules:
  0.0 70.2 jit_solution(15679073379227123457)
XLA Ops:
  0.6 67.0 %ffn_backward.1 = (bf16[32,1024]{1,0:T(8,128)(2,1)}, f32[64,1024]{1,0:T(8,128)}, bf16[8,64,1024]{2,1,0:T(8,128)(2,1)}) custom-call(bf16[256,1024]{1,0:T(8,128)(2,1)} %refs_0_.1, bf16[256,1024]{1,0:T(8,128)(2,1)} %refs_1_.1, bf16[3696,1024]{1,0:T(8,128)(2,1)} %bitcast.5, bf16[3696,1024]{1,0:T(8,128)(2,1)} %bitcast.6, bf16[3696,1024]{1,0:T(8,128)(2,1)} %refs_4_.1, ...), custom_call_target="tpu_custom_call" | custom-call | tf_op jit(solution)/shard_map/ffn_backward/pallas_call | solution.py:515
  67.7 2.5 %write_out.1 = (bf16[32,1024]{1,0:T(8,128)(2,1)}, f32[64,1024]{1,0:T(8,128)}, f32[8,64,1024]{2,1,0:T(8,128)}) custom-call(bf16[32,1024]{1,0:T(8,128)(2,1)} %get-tuple-element.9.x_in, f32[64,1024]{1,0:T(8,128)} %get-tuple-element.10.shared_in, bf16[8,64,1024]{2,1,0:T(8,128)(2,1)} %get-tuple-element.11.heads_in), custom_call_target="tpu_custom_call" | custom-call | tf_op jit(solution)/shard_map/write_out/pallas_call | solution.py:534

commit v6 on v5

--- a/solution.py
+++ b/solution.py
@@ -379,9 +379,9 @@
             spread(main, j)
 
         stage(0, matmul_stage)
-        once(0, special_matmul_stage)
         stage(LAG_ADD, lambda j: add(main, j))
-        once(LAG_ADD, lambda: add(special, 0))
+        once(LAG_ADD, special_matmul_stage)
+        once(LAG_ADD + 1, lambda: add(special, 0))
         stage(LAG_RELAY, lambda j: relay(main, j))
         once(LAG_RELAY, lambda: relay(special, 0))
         stage(LAG_GRAD, grad_stage)

time: 70.4 us -> 70.6 us (level)
  no operation moved by 1% of the time
where the time goes in v6:
time: 70.6 us; the launch traced here: 70.5 us
  Pallas kernels  69.9 us (99%)
    pallas_call x1, Pallas kernels, step(): pl.pallas_call(kernel, out_shape=(jax.ShapeDtypeStruct((32, width), BF16)...  67.4 us
    pallas_call x1, Pallas kernels, step(): pl.pallas_call(finish, out_shape=(jax.ShapeDtypeStruct(made[0].shape, BF1...  2.5 us

profile of v6, /device:TPU:0, one launch (start us, length us, event | category | flops | bytes accessed | tf_op | source)
XLA Modules:
  0.0 70.5 jit_solution(14036715868589830854)
XLA Ops:
  0.6 67.4 %ffn_backward.1 = (bf16[32,1024]{1,0:T(8,128)(2,1)}, f32[64,1024]{1,0:T(8,128)}, bf16[8,64,1024]{2,1,0:T(8,128)(2,1)}) custom-call(bf16[256,1024]{1,0:T(8,128)(2,1)} %refs_0_.1, bf16[256,1024]{1,0:T(8,128)(2,1)} %refs_1_.1, bf16[3696,1024]{1,0:T(8,128)(2,1)} %bitcast.5, bf16[3696,1024]{1,0:T(8,128)(2,1)} %bitcast.6, bf16[3696,1024]{1,0:T(8,128)(2,1)} %refs_4_.1, ...), custom_call_target="tpu_custom_call" | custom-call | tf_op jit(solution)/shard_map/ffn_backward/pallas_call | solution.py:515
  68.0 2.5 %write_out.1 = (bf16[32,1024]{1,0:T(8,128)(2,1)}, f32[64,1024]{1,0:T(8,128)}, f32[8,64,1024]{2,1,0:T(8,128)}) custom-call(bf16[32,1024]{1,0:T(8,128)(2,1)} %get-tuple-element.9.x_in, f32[64,1024]{1,0:T(8,128)} %get-tuple-element.10.shared_in, bf16[8,64,1024]{2,1,0:T(8,128)(2,1)} %get-tuple-element.11.heads_in), custom_call_target="tpu_custom_call" | custom-call | tf_op jit(solution)/shard_map/write_out/pallas_call | solution.py:534
